TPU v7x, 32 devices: a whole 2x2x4 slice. The times are simulated.
32 devices in a mesh: orb: 8 (over z, x), grid: 4 (over y, core).
Axes of the slice: x: 2, y: 2, z: 4, core: 2. Of those that a mesh axis runs over, the one named last changes fastest.
Arguments:
- potentials: float32 [8, 2, 4, 64, 1024], P('orb', None, None, 'grid'), may hold values from -6 to 6
- orbitals: float32 [32, 64, 1024], P('orb', 'grid'), may hold values from -6 to 6
- local_pot: float32 [64, 1024], P('grid'), may hold values from 0 to 1
- shifts: float32 [32], P('orb'), may hold values from 0.75 to 2
- occupation: int32 [32], P('orb'), may hold values from 1 to 2
- owner: int32 [2], replicated, may hold values from 0 to 7
Outputs:
- response: float32 [8, 2, 4, 64, 1024], P('orb', None, None, 'grid')
All inputs are finite; a program needn't handle non-finite values.
Results may differ from a plain program's by a relative error of at most 0.00002.
Values sent between devices are 32-bit elements; how exact they have to be, the bound alone decides.
A program may use at most 64 MiB of HBM per device.

v0:
```python
import jax
import jax.numpy as jnp
from jax import lax
from jax.sharding import PartitionSpec as P

NZ = 32
ITERS = 4
NEAR_COEF = 4.0 / 3.0
FAR_COEF = -1.0 / 12.0
CENTER_COEF = -2.5
KINETIC_DIAG = 3.75


def with_halo(cells, sides, width):
    for axis, dim in sides:
        count = lax.axis_size(axis)
        ends = count - 1
        head = lax.slice_in_dim(cells, 0, width, axis=dim)
        tail = lax.slice_in_dim(cells, cells.shape[dim] - width, cells.shape[dim], axis=dim)
        cells = jnp.concatenate(
            [
                lax.ppermute(tail, axis, [(i, (i + 1) % count) for i in range(ends)]),
                cells,
                lax.ppermute(head, axis, [((i + 1) % count, i) for i in range(ends)]),
            ],
            axis=dim,
        )
    return cells


def from_root(value, axis, source):
    kept = jnp.where(lax.axis_index(axis) == source, value, 0).astype(value.dtype)
    return lax.psum(kept, axis)


def laplacian(padded, solution):
    cell_rows = solution.shape[-2]
    plane_cells = solution.shape[-1]
    along_rows = NEAR_COEF * (
        padded[..., 1 : cell_rows + 1, :] + padded[..., 3 : cell_rows + 3, :]
    ) + FAR_COEF * (padded[..., 0:cell_rows, :] + padded[..., 4 : cell_rows + 4, :])
    widths = [(0, 0)] * (solution.ndim - 1)
    padded_cols = jnp.pad(solution, widths + [(2 * NZ, 2 * NZ)])
    along_cols = NEAR_COEF * (
        padded_cols[..., NZ : NZ + plane_cells] + padded_cols[..., 3 * NZ : 3 * NZ + plane_cells]
    ) + FAR_COEF * (
        padded_cols[..., 0:plane_cells] + padded_cols[..., 4 * NZ : 4 * NZ + plane_cells]
    )
    padded_depth = jnp.pad(solution, widths + [(2, 2)])
    z_index = jnp.arange(plane_cells, dtype=jnp.int32) % NZ
    lower_one = (z_index >= 1).astype(solution.dtype)
    upper_one = (z_index <= NZ - 2).astype(solution.dtype)
    lower_two = (z_index >= 2).astype(solution.dtype)
    upper_two = (z_index <= NZ - 3).astype(solution.dtype)
    along_depth = NEAR_COEF * (
        padded_depth[..., 1 : plane_cells + 1] * lower_one
        + padded_depth[..., 3 : plane_cells + 3] * upper_one
    ) + FAR_COEF * (
        padded_depth[..., 0:plane_cells] * lower_two
        + padded_depth[..., 4 : plane_cells + 4] * upper_two
    )
    return along_rows + along_cols + along_depth + 3.0 * CENTER_COEF * solution


def sweep(padded, solution, source, potential, diagonal):
    applied = -0.5 * laplacian(padded, solution) + potential * solution
    return solution + (source - applied) / diagonal


def shards(potentials, orbitals, local_pot, shifts, occupation, owner):
    cell_rows = orbitals.shape[1]
    orbital_count = orbitals.shape[0]
    position = lax.axis_index("orb")
    weights = occupation.astype(jnp.float32)
    stored = potentials[0]
    block_count = stored.shape[0]
    results = []
    for block_index in range(block_count):
        trials = from_root(stored[block_index], "orb", owner[block_index])
        halo_depth = 2 * ITERS
        trial_count = trials.shape[0]
        stacked = jnp.concatenate([orbitals, trials, local_pot[None]], axis=0)
        extended = with_halo(stacked, (("grid", 1),), halo_depth)
        orbit_ext = extended[:orbital_count]
        trial_ext = extended[orbital_count : orbital_count + trial_count]
        local_ext = extended[orbital_count + trial_count]
        source_ext = -(trial_ext[None] * orbit_ext[:, None])
        potential_ext = local_ext[None, None] + shifts[:, None, None, None]
        diagonal_ext = KINETIC_DIAG + potential_ext
        global_rows = (
            lax.axis_index("grid") * cell_rows
            - halo_depth
            + jnp.arange(cell_rows + 2 * halo_depth, dtype=jnp.int32)
        )
        inside = ((global_rows >= 0) & (global_rows < cell_rows * lax.axis_size("grid"))).astype(
            jnp.float32
        )[:, None]
        solution_ext = source_ext / diagonal_ext
        for repeat in range(ITERS):
            margin = 2 * (repeat + 1)
            extent = cell_rows + 2 * halo_depth - 2 * margin
            center = solution_ext[:, :, 2 : 2 + extent]
            source_cut = source_ext[:, :, margin : margin + extent]
            potential_cut = potential_ext[:, :, margin : margin + extent]
            diagonal_cut = diagonal_ext[:, :, margin : margin + extent]
            inside_cut = inside[margin : margin + extent]
            solution_ext = (
                sweep(solution_ext, center, source_cut, potential_cut, diagonal_cut) * inside_cut
            )
        results.append(
            lax.psum(
                jnp.sum(weights[:, None, None, None] * orbitals[:, None] * solution_ext, axis=0),
                "orb",
            )
        )
    totals = jnp.stack(results, 0)
    owned = (owner == position).astype(jnp.float32)
    return (owned[:, None, None, None] * totals)[None]


def solution(mesh):
    in_specs = (
        P("orb", None, None, "grid", None),
        P("orb", "grid", None),
        P("grid", None),
        P("orb"),
        P("orb"),
        P(),
    )
    out_specs = P("orb", None, None, "grid", None)
    return jax.shard_map(shards, mesh=mesh, in_specs=in_specs, out_specs=out_specs, check_vma=False)
```

profile of v0, /device:TPU:0, one launch (start us, length us, event | category | flops | bytes accessed | tf_op | source)
XLA Modules:
  0.0 220.6 jit_solution(12964091721920774921)
XLA Ops:
  6.5 0.0 copy-start.6
  6.5 0.0 copy-start.3
  6.5 0.0 copy-start
  6.5 0.0 all-reduce.23.cloned.1.call-start
  6.5 1.4 fusion.225
  9.2 1.9 select_bitcast_fusion.1
  11.1 0.0 all-reduce.23.cloned.1.call-update
  11.1 0.0 all-reduce.21.cloned.1.call-start
  11.1 0.1 slice.471
  11.2 0.1 slice.488
  11.3 0.1 slice.505
  11.4 0.1 slice.522
  11.4 0.0 copy-done.6
  11.4 75.5 %all-reduce.23.cloned.1.call-done = (f32[4,16,1024]{2,1,0:T(8,128)}, f32[4,16,1024]{2,1,0:T(8,128)}) async-done(((f32[4,16,1024]{2,1,0:T(8,128)}, f32[4,16,1024]{2,1,0:T(8,128)}), (f32[4,16,1024]{2,1,0:T(8,128)}, f32[4,16,1024]{2,1,0:T(8,128)})) %all-reduce.23.cloned.1.call-update) | async-done | bytes 524304 | tf_op jit(solution)/shard_map/psum | solution.py:33
  86.9 0.0 copy-done.3
  86.9 0.0 copy-done
  87.0 1.2 pad_maximum_fusion.5
  88.1 0.0 copy-start.1
  88.1 0.0 copy-start.2
  88.2 1.4 collective-permute-start
  89.6 1.3 collective-permute-start.1
  91.0 4.7 %collective-permute-start.2 = (f32[9,8,1024]{2,1,0:T(8,128)S(1)}, f32[9,8,1024]{2,1,0:T(8,128)S(1)}, u32[]{:S(2)}, u32[]{:S(2)}) collective-permute-start(f32[9,8,1024]{2,1,0:T(8,128)S(1)} %get-tuple-element.19), channel_id=1, source_target_pairs={{0,1},{1,2},{2,3},{4,5},{5,6},{6,7},{8,9},{9,10},{10,11},{12,13},{... | collective-permute-start | bytes 884744 | tf_op jit(solution)/shard_map/ppermute | solution.py:22
  95.7 1.3 collective-permute-start.3
  97.0 0.1 broadcast_multiply_fusion
  97.1 0.0 collective-permute-done
  97.1 0.0 collective-permute-done.1
  97.1 0.0 collective-permute-done.2
  97.2 3.3 %collective-permute-done.3 = f32[9,8,1024]{2,1,0:T(8,128)S(1)} collective-permute-done((f32[9,8,1024]{2,1,0:T(8,128)S(1)}, f32[9,8,1024]{2,1,0:T(8,128)S(1)}, u32[]{:S(2)}, u32[]{:S(2)}) %collective-permute-start.3) | collective-permute-done | bytes 294944 | tf_op jit(solution)/shard_map/ppermute | solution.py:24
  100.4 0.0 copy-done.1
  100.4 0.0 copy-done.2
  100.4 0.2 fusion.157
  100.7 0.0 copy-start.4
  100.7 0.1 fusion.221
  100.9 0.5 copy-done.4
  101.4 0.2 add_add_fusion.1
  101.5 0.3 broadcast_add_fusion.3
  101.9 0.1 slice_bitcast_fusion.2
  102.0 0.1 slice_bitcast_fusion.3
  102.2 0.1 slice_bitcast_fusion
  102.4 0.1 slice_bitcast_fusion.1
  102.6 0.6 multiply_negate_fusion.1
  103.2 0.4 slice.599
  103.6 4.8 %fusion.51 = f32[4,4,28,1024]{3,2,1,0:T(8,128)S(1)} fusion(f32[4,4,28,1024]{3,2,1,0:T(8,128)S(1)} %slice.599, f32[4,4,32,1024]{3,2,1,0:T(8,128)S(1)} %get-tuple-element.14, f32[4,4,32,1024]{3,2,1,0:T(8,128)S(1)} %get-tuple-element.13, f32[28]{0:T(128)S(1)} %slice.471, f32[4,28,1024]{2,1,0:T(8,128)S(1)} %slice_bitcast_fusion.2, ...), kind=kLoop, calls=%fused_computation.73 | loop fusion | flops 13762560 | bytes 13779056 | tf_op jit(solution)/shard_map/mul | solution.py:108
  108.4 0.2 slice.607
  108.6 3.5 %fusion.155 = f32[4,4,24,1024]{3,2,1,0:T(8,128)S(1)} fusion(f32[4,4,24,1024]{3,2,1,0:T(8,128)S(1)} %slice.607, f32[4,4,28,1024]{3,2,1,0:T(8,128)S(1)} %fusion.51, f32[4,4,32,1024]{3,2,1,0:T(8,128)S(1)} %get-tuple-element.13, f32[24]{0:T(128)S(1)} %slice.488, f32[4,24,1024]{2,1,0:T(8,128)S(1)} %slice_bitcast_fusion.10, ...), kind=kLoop, calls=%fused_computation.219 | loop fusion | flops 11796480 | bytes 11812960 | tf_op jit(solution)/shard_map/mul | solution.py:108
  112.2 0.2 slice.615
  112.4 3.5 %fusion.154 = f32[4,4,20,1024]{3,2,1,0:T(8,128)S(1)} fusion(f32[4,4,20,1024]{3,2,1,0:T(8,128)S(1)} %slice.615, f32[4,4,24,1024]{3,2,1,0:T(8,128)S(1)} %fusion.155, f32[4,4,32,1024]{3,2,1,0:T(8,128)S(1)} %get-tuple-element.13, f32[20]{0:T(128)S(1)} %slice.505, f32[4,20,1024]{2,1,0:T(8,128)S(1)} %slice_bitcast_fusion.8, ...), kind=kLoop, calls=%fused_computation.218 | loop fusion | flops 9830400 | bytes 9846864 | tf_op jit(solution)/shard_map/mul | solution.py:108
  115.9 0.2 slice.623
  116.1 0.6 multiply_negate_fusion
  116.6 0.4 slice.636
  117.1 4.6 %fusion.50 = f32[4,4,28,1024]{3,2,1,0:T(8,128)S(1)} fusion(f32[4,4,28,1024]{3,2,1,0:T(8,128)S(1)} %slice.636, f32[4,4,32,1024]{3,2,1,0:T(8,128)S(1)} %get-tuple-element.16, f32[4,4,32,1024]{3,2,1,0:T(8,128)S(1)} %get-tuple-element.15, f32[4,28,1024]{2,1,0:T(8,128)S(1)} %slice_bitcast_fusion, f32[4,28,1024]{2,1,0:T(8,128)S(1)} %slice_bitcast_fusion.1, ...), kind=kLoop, calls=%fused_computation.72 | loop fusion | flops 13762560 | bytes 13779056 | tf_op jit(solution)/shard_map/mul | solution.py:108
  121.7 0.2 slice.644
  121.9 3.5 %fusion.153 = f32[4,4,24,1024]{3,2,1,0:T(8,128)S(1)} fusion(f32[4,4,24,1024]{3,2,1,0:T(8,128)S(1)} %slice.644, f32[4,4,28,1024]{3,2,1,0:T(8,128)S(1)} %fusion.50, f32[4,4,32,1024]{3,2,1,0:T(8,128)S(1)} %get-tuple-element.15, f32[4,24,1024]{2,1,0:T(8,128)S(1)} %slice_bitcast_fusion.6, f32[4,24,1024]{2,1,0:T(8,128)S(1)} %slice_bitcast_fusion.7, ...), kind=kLoop, calls=%fused_computation.217 | loop fusion | flops 11796480 | bytes 11812960 | tf_op jit(solution)/shard_map/mul | solution.py:108
  125.4 0.3 slice.652
  125.7 3.7 %fusion.152 = f32[4,4,20,1024]{3,2,1,0:T(8,128)S(1)} fusion(f32[4,4,20,1024]{3,2,1,0:T(8,128)S(1)} %slice.652, f32[4,4,24,1024]{3,2,1,0:T(8,128)S(1)} %fusion.153, f32[4,4,32,1024]{3,2,1,0:T(8,128)S(1)} %get-tuple-element.15, f32[4,20,1024]{2,1,0:T(8,128)S(1)} %slice_bitcast_fusion.4, f32[4,20,1024]{2,1,0:T(8,128)S(1)} %slice_bitcast_fusion.5, ...), kind=kLoop, calls=%fused_computation.216 | loop fusion | flops 9830400 | bytes 9846864 | tf_op jit(solution)/shard_map/mul | solution.py:108
  129.4 0.1 slice.660
  129.5 3.1 %multiply_reduce_fusion.1 = f32[4,16,1024]{2,1,0:T(8,128)} fusion(f32[4,4,16,1024]{3,2,1,0:T(8,128)S(1)} %slice.623, f32[4,4,20,1024]{3,2,1,0:T(8,128)S(1)} %fusion.154, f32[4,4,32,1024]{3,2,1,0:T(8,128)S(1)} %get-tuple-element.13, f32[16]{0:T(128)S(1)} %slice.522, f32[4,16,1024]{2,1,0:T(8,128)S(1)} %slice_bitcast_fusion.14, ...), kind=kLoop, calls=%fused_computation.298 | loop fusion | flops 8323072 | bytes 7356480 | tf_op jit(solution)/shard_map/reduce_sum | solution.py:112
  132.7 0.0 copy-start.5
  132.7 3.1 %multiply_reduce_fusion = f32[4,16,1024]{2,1,0:T(8,128)} fusion(f32[4,4,16,1024]{3,2,1,0:T(8,128)S(1)} %slice.660, f32[4,4,20,1024]{3,2,1,0:T(8,128)S(1)} %fusion.152, f32[4,4,32,1024]{3,2,1,0:T(8,128)S(1)} %get-tuple-element.15, f32[4,16,1024]{2,1,0:T(8,128)S(1)} %slice_bitcast_fusion.12, f32[4,16,1024]{2,1,0:T(8,128)S(1)} %slice_bitcast_fusion.13, ...), kind=kLoop, calls=%fused_computation.296 | loop fusion | flops 8323072 | bytes 7356480 | tf_op jit(solution)/shard_map/reduce_sum | solution.py:112
  135.8 0.0 all-reduce.21.cloned.1.call-update
  135.8 0.0 copy-done.5
  135.8 76.0 %all-reduce.21.cloned.1.call-done = (f32[1,1,4,16,1024]{4,3,2,1,0:T(8,128)}, f32[1,1,4,16,1024]{4,3,2,1,0:T(8,128)}) async-done(((f32[1,1,4,16,1024]{4,3,2,1,0:T(8,128)}, f32[1,1,4,16,1024]{4,3,2,1,0:T(8,128)}), (f32[1,1,4,16,1024]{4,3,2,1,0:T(8,128)}, f32[1,1,4,16,1024]{4,3,2,1,0:T(8,128)})) %all-reduce.21.cloned.1.call-update) | async-done | bytes 524304 | tf_op jit(solution)/shard_map/psum | solution.py:111
  211.8 1.9 maximum_multiply_fusion
  (20 shorter events, 0.5 us)
Async XLA Ops:
  6.5 4.9 %copy-start.6 = (s32[4]{0:T(128)S(1)}, s32[4]{0:T(128)}, u32[]{:S(2)}) copy-start(s32[4]{0:T(128)} %param.10) | copy-start | bytes 52
  6.5 80.4 %copy-start.3 = (f32[16,1024]{1,0:T(8,128)S(1)}, f32[16,1024]{1,0:T(8,128)}, u32[]{:S(2)}) copy-start(f32[16,1024]{1,0:T(8,128)} %param.8) | copy-start | bytes 196612
  6.5 80.4 %copy-start = (f32[4,16,1024]{2,1,0:T(8,128)S(1)}, f32[4,16,1024]{2,1,0:T(8,128)}, u32[]{:S(2)}) copy-start(f32[4,16,1024]{2,1,0:T(8,128)} %param.7) | copy-start | bytes 786436
  6.5 80.4 %all-reduce.23.cloned.1.call-start = ((), (), s32[]{:S(2)}) async-start(), calls=%async_computation.1 | async-start | bytes 1048576 | tf_op jit(solution)/shard_map/psum | solution.py:33
  11.1 200.8 %all-reduce.21.cloned.1.call-start = ((), (), s32[]{:S(2)}) async-start(), calls=%async_computation | async-start | bytes 1048576 | tf_op jit(solution)/shard_map/psum | solution.py:111
  88.1 12.3 %copy-start.1 = (f32[4,16,1024]{2,1,0:T(8,128)S(1)}, f32[4,16,1024]{2,1,0:T(8,128)}, u32[]{:S(2)}) copy-start(f32[4,16,1024]{2,1,0:T(8,128)} %get-tuple-element.7) | copy-start | bytes 786436
  88.1 12.3 %copy-start.2 = (f32[4,16,1024]{2,1,0:T(8,128)S(1)}, f32[4,16,1024]{2,1,0:T(8,128)}, u32[]{:S(2)}) copy-start(f32[4,16,1024]{2,1,0:T(8,128)} %get-tuple-element.8) | copy-start | bytes 786436
  88.2 9.0 %collective-permute-start = (f32[9,8,1024]{2,1,0:T(8,128)S(1)}, f32[9,8,1024]{2,1,0:T(8,128)S(1)}, u32[]{:S(2)}, u32[]{:S(2)}) collective-permute-start(f32[9,8,1024]{2,1,0:T(8,128)S(1)} %get-tuple-element.17), channel_id=1, source_target_pairs={{0,1},{1,2},{2,3},{4,5},{5,6},{6,7},{8,9},{9,10},{10,11},{12,13},{... | collective-permute-start | bytes 884744 | tf_op jit(solution)/shard_map/ppermute | solution.py:22
  89.6 7.5 %collective-permute-start.1 = (f32[9,8,1024]{2,1,0:T(8,128)S(1)}, f32[9,8,1024]{2,1,0:T(8,128)S(1)}, u32[]{:S(2)}, u32[]{:S(2)}) collective-permute-start(f32[9,8,1024]{2,1,0:T(8,128)S(1)} %get-tuple-element.18), channel_id=1, source_target_pairs={{1,0},{2,1},{3,2},{5,4},{6,5},{7,6},{9,8},{10,9},{11,10},{13,12},{... | collective-permute-start | bytes 884744 | tf_op jit(solution)/shard_map/ppermute | solution.py:24
  91.0 6.2 %collective-permute-start.2 = (f32[9,8,1024]{2,1,0:T(8,128)S(1)}, f32[9,8,1024]{2,1,0:T(8,128)S(1)}, u32[]{:S(2)}, u32[]{:S(2)}) collective-permute-start(f32[9,8,1024]{2,1,0:T(8,128)S(1)} %get-tuple-element.19), channel_id=1, source_target_pairs={{0,1},{1,2},{2,3},{4,5},{5,6},{6,7},{8,9},{9,10},{10,11},{12,13},{... | collective-permute-start | bytes 884744 | tf_op jit(solution)/shard_map/ppermute | solution.py:22
  95.7 4.7 %collective-permute-start.3 = (f32[9,8,1024]{2,1,0:T(8,128)S(1)}, f32[9,8,1024]{2,1,0:T(8,128)S(1)}, u32[]{:S(2)}, u32[]{:S(2)}) collective-permute-start(f32[9,8,1024]{2,1,0:T(8,128)S(1)} %get-tuple-element.20), channel_id=1, source_target_pairs={{1,0},{2,1},{3,2},{5,4},{6,5},{7,6},{9,8},{10,9},{11,10},{13,12},{... | collective-permute-start | bytes 884744 | tf_op jit(solution)/shard_map/ppermute | solution.py:24
  100.7 0.7 copy-start.4
  132.7 3.1 %copy-start.5 = (s32[2]{0:T(128)S(1)}, s32[2]{0:T(128)}, u32[]{:S(2)}) copy-start(s32[2]{0:T(128)} %param.11) | copy-start | bytes 28
Sparse Core Ops, SparseCore 0:
  11.2 75.7 all-reduce.22
  135.9 75.8 all-reduce.20
where the time goes:
time: 221 us
  waiting for transfers between devices  155 us (70%)
  other arithmetic  36.9 us (17%)
  between operations  15.1 us (7%)
  starting transfers between devices  8.81 us (4%)
  local copies, waits for them, and re-layouts  5.03 us (2%)
    psum x1, waiting for transfers between devices, shards(): lax.psum(jnp.sum(weights[:, None, None, None] * orbitals[:, None] * solut...  76 us
    psum x1, waiting for transfers between devices, from_root(): return lax.psum(kept, axis)  75.5 us
    mul x6, other arithmetic, shards(): sweep(solution_ext, center, source_cut, potential_cut, diagonal_cut)  23.7 us
    reduce_sum x2, other arithmetic, shards(): jnp.sum(weights[:, None, None, None] * orbitals[:, None] * solution_ext,...  6.25 us
    ppermute x2, starting transfers between devices, with_halo(): lax.ppermute(tail, axis, [(i, (i + 1) % count) for i in range(ends)])  6.18 us
  transfers between devices with their start and end apart: 6, of which 3 were waited for; matrix products, arithmetic and copies ran while one was open for 0% of the time, Pallas kernels for 0%

commit v1 on v0

--- a/solution.py
+++ b/solution.py
@@ -9,6 +9,11 @@
 FAR_COEF = -1.0 / 12.0
 CENTER_COEF = -2.5
 KINETIC_DIAG = 3.75
+
+
+def scan_roads_all(matrix, chip_axis):
+    v1 = jnp.sum(lax.all_gather(matrix, axis_name=chip_axis), axis=0)
+    return v1
 
 
 def with_halo(cells, sides, width):
@@ -30,7 +35,7 @@
 
 def from_root(value, axis, source):
     kept = jnp.where(lax.axis_index(axis) == source, value, 0).astype(value.dtype)
-    return lax.psum(kept, axis)
+    return scan_roads_all(kept, axis)
 
 
 def laplacian(padded, solution):

time: 221 us -> 246 us (1.11)
  waiting for transfers between devices: 155 us -> 178 us
    all_gather x0 -> x2, waiting for transfers between devices: none -> 98.8 us  [scan_roads_all(): v1 = jnp.sum(lax.all_gather(matrix, axis_name=chip_axis), axis=0)]
    psum x1 -> x0, waiting for transfers between devices: 75.5 us -> none  [from_root(): return lax.psum(kept, axis)]
    reduce_sum x0 -> x2, other arithmetic: none -> 3.49 us  [scan_roads_all(): v1 = jnp.sum(lax.all_gather(matrix, axis_name=chip_axis), axis=0)]
  transfers between devices with their start and end apart: 6 -> 7, of which waited for: 3 -> 4; matrix products, arithmetic and copies ran while one was open for 0% -> 1% of each run, Pallas kernels for 0% -> 0%
where the time goes in v1:
time: 246 us
  waiting for transfers between devices  178 us (72%)
  other arithmetic  39.3 us (16%)
  between operations  14.9 us (6%)
  starting transfers between devices  8.71 us (4%)
  local copies, waits for them, and re-layouts  5.08 us (2%)
    all_gather x2, waiting for transfers between devices, scan_roads_all(): v1 = jnp.sum(lax.all_gather(matrix, axis_name=chip_axis), axis=0)  98.8 us
    psum x1, waiting for transfers between devices, shards(): lax.psum(jnp.sum(weights[:, None, None, None] * orbitals[:, None] * solut...  75.3 us
    mul x6, other arithmetic, shards(): sweep(solution_ext, center, source_cut, potential_cut, diagonal_cut)  23.6 us
    reduce_sum x2, other arithmetic, shards(): jnp.sum(weights[:, None, None, None] * orbitals[:, None] * solution_ext,...  6.24 us
    ppermute x2, starting transfers between devices, with_halo(): lax.ppermute(tail, axis, [(i, (i + 1) % count) for i in range(ends)])  6.04 us
  transfers between devices with their start and end apart: 7, of which 4 were waited for; matrix products, arithmetic and copies ran while one was open for 1% of the time, Pallas kernels for 0%

profile of v1, /device:TPU:0, one launch (start us, length us, event | category | flops | bytes accessed | tf_op | source)
XLA Modules:
  0.0 246.2 jit_solution(9486669123672844221)
XLA Ops:
  6.5 0.0 copy-start.4
  6.5 0.0 all-gather.5.cloned.1.call-start
  6.5 1.4 fusion.225
  9.3 1.9 slice_select_fusion.1
  11.2 0.0 all-gather.5.cloned.1.call-update
  11.2 0.0 all-gather.7.cloned.1.call-start
  11.2 0.7 all-gather.7.cloned.1.call-update
  11.9 0.0 all-reduce.19.cloned.1.call-start
  12.0 0.1 slice.471
  12.1 0.1 slice.488
  12.1 0.1 slice.505
  12.2 0.1 slice.522
  12.3 0.0 copy-done.4
  12.3 50.8 %all-gather.5.cloned.1.call-done = f32[8,1,4,16,1024]{4,3,2,1,0:T(8,128)} async-done(((f32[1,1,4,16,1024]{4,3,2,1,0:T(8,128)}), f32[8,1,4,16,1024]{4,3,2,1,0:T(8,128)}) %all-gather.5.cloned.1.call-update) | async-done | bytes 2097168 | tf_op jit(solution)/shard_map/all_gather | solution.py:15
  63.1 1.7 reduce_sum.36
  64.9 0.0 copy-start
  64.9 0.0 copy-start.1
  64.9 48.0 %all-gather.7.cloned.1.call-done = f32[8,1,4,16,1024]{4,3,2,1,0:T(8,128)} async-done(((f32[1,1,4,16,1024]{4,3,2,1,0:T(8,128)}), f32[8,1,4,16,1024]{4,3,2,1,0:T(8,128)}) %all-gather.7.cloned.1.call-update) | async-done | bytes 2097168 | tf_op jit(solution)/shard_map/all_gather | solution.py:15
  112.9 1.7 reduce_sum.38
  114.7 0.0 copy-done
  114.7 0.0 copy-done.1
  114.7 0.1 pad_maximum_fusion.5
  114.9 1.3 collective-permute-start
  116.2 1.3 collective-permute-start.1
  117.5 4.7 %collective-permute-start.2 = (f32[9,8,1024]{2,1,0:T(8,128)S(1)}, f32[9,8,1024]{2,1,0:T(8,128)S(1)}, u32[]{:S(2)}, u32[]{:S(2)}) collective-permute-start(f32[9,8,1024]{2,1,0:T(8,128)S(1)} %get-tuple-element.17), channel_id=1, source_target_pairs={{0,1},{1,2},{2,3},{4,5},{5,6},{6,7},{8,9},{9,10},{10,11},{12,13},{... | collective-permute-start | bytes 884744 | tf_op jit(solution)/shard_map/ppermute | solution.py:27
  122.3 1.3 collective-permute-start.3
  123.6 0.1 broadcast_multiply_fusion
  123.7 0.0 collective-permute-done
  123.7 0.0 collective-permute-done.1
  123.7 0.0 collective-permute-done.2
  123.7 3.3 %collective-permute-done.3 = f32[9,8,1024]{2,1,0:T(8,128)S(1)} collective-permute-done((f32[9,8,1024]{2,1,0:T(8,128)S(1)}, f32[9,8,1024]{2,1,0:T(8,128)S(1)}, u32[]{:S(2)}, u32[]{:S(2)}) %collective-permute-start.3) | collective-permute-done | bytes 294944 | tf_op jit(solution)/shard_map/ppermute | solution.py:29
  127.0 0.3 fusion.157
  127.3 0.0 copy-start.2
  127.3 0.2 fusion.221
  127.5 0.4 copy-done.2
  127.9 0.2 add_add_fusion.1
  128.1 0.3 broadcast_add_fusion.3
  128.5 0.1 slice_bitcast_fusion.2
  128.6 0.1 slice_bitcast_fusion.3
  128.8 0.1 slice_bitcast_fusion
  128.9 0.1 slice_bitcast_fusion.1
  129.2 0.6 multiply_negate_fusion.1
  129.8 0.4 slice.599
  130.2 4.8 %fusion.51 = f32[4,4,28,1024]{3,2,1,0:T(8,128)S(1)} fusion(f32[4,4,28,1024]{3,2,1,0:T(8,128)S(1)} %slice.599, f32[4,4,32,1024]{3,2,1,0:T(8,128)S(1)} %get-tuple-element.12, f32[4,4,32,1024]{3,2,1,0:T(8,128)S(1)} %get-tuple-element.11, f32[28]{0:T(128)S(1)} %slice.471, f32[4,28,1024]{2,1,0:T(8,128)S(1)} %slice_bitcast_fusion.2, ...), kind=kLoop, calls=%fused_computation.73 | loop fusion | flops 13762560 | bytes 13779056 | tf_op jit(solution)/shard_map/mul | solution.py:113
  135.0 0.3 slice.607
  135.3 3.5 %fusion.155 = f32[4,4,24,1024]{3,2,1,0:T(8,128)S(1)} fusion(f32[4,4,24,1024]{3,2,1,0:T(8,128)S(1)} %slice.607, f32[4,4,28,1024]{3,2,1,0:T(8,128)S(1)} %fusion.51, f32[4,4,32,1024]{3,2,1,0:T(8,128)S(1)} %get-tuple-element.11, f32[24]{0:T(128)S(1)} %slice.488, f32[4,24,1024]{2,1,0:T(8,128)S(1)} %slice_bitcast_fusion.10, ...), kind=kLoop, calls=%fused_computation.219 | loop fusion | flops 11796480 | bytes 11812960 | tf_op jit(solution)/shard_map/mul | solution.py:113
  138.8 0.2 slice.615
  139.0 3.5 %fusion.154 = f32[4,4,20,1024]{3,2,1,0:T(8,128)S(1)} fusion(f32[4,4,20,1024]{3,2,1,0:T(8,128)S(1)} %slice.615, f32[4,4,24,1024]{3,2,1,0:T(8,128)S(1)} %fusion.155, f32[4,4,32,1024]{3,2,1,0:T(8,128)S(1)} %get-tuple-element.11, f32[20]{0:T(128)S(1)} %slice.505, f32[4,20,1024]{2,1,0:T(8,128)S(1)} %slice_bitcast_fusion.8, ...), kind=kLoop, calls=%fused_computation.218 | loop fusion | flops 9830400 | bytes 9846864 | tf_op jit(solution)/shard_map/mul | solution.py:113
  142.5 0.2 slice.623
  142.7 0.6 multiply_negate_fusion
  143.3 0.4 slice.636
  143.7 4.6 %fusion.50 = f32[4,4,28,1024]{3,2,1,0:T(8,128)S(1)} fusion(f32[4,4,28,1024]{3,2,1,0:T(8,128)S(1)} %slice.636, f32[4,4,32,1024]{3,2,1,0:T(8,128)S(1)} %get-tuple-element.14, f32[4,4,32,1024]{3,2,1,0:T(8,128)S(1)} %get-tuple-element.13, f32[4,28,1024]{2,1,0:T(8,128)S(1)} %slice_bitcast_fusion, f32[4,28,1024]{2,1,0:T(8,128)S(1)} %slice_bitcast_fusion.1, ...), kind=kLoop, calls=%fused_computation.72 | loop fusion | flops 13762560 | bytes 13779056 | tf_op jit(solution)/shard_map/mul | solution.py:113
  148.3 0.2 slice.644
  148.5 3.5 %fusion.153 = f32[4,4,24,1024]{3,2,1,0:T(8,128)S(1)} fusion(f32[4,4,24,1024]{3,2,1,0:T(8,128)S(1)} %slice.644, f32[4,4,28,1024]{3,2,1,0:T(8,128)S(1)} %fusion.50, f32[4,4,32,1024]{3,2,1,0:T(8,128)S(1)} %get-tuple-element.13, f32[4,24,1024]{2,1,0:T(8,128)S(1)} %slice_bitcast_fusion.6, f32[4,24,1024]{2,1,0:T(8,128)S(1)} %slice_bitcast_fusion.7, ...), kind=kLoop, calls=%fused_computation.217 | loop fusion | flops 11796480 | bytes 11812960 | tf_op jit(solution)/shard_map/mul | solution.py:113
  152.0 0.2 slice.652
  152.3 3.7 %fusion.152 = f32[4,4,20,1024]{3,2,1,0:T(8,128)S(1)} fusion(f32[4,4,20,1024]{3,2,1,0:T(8,128)S(1)} %slice.652, f32[4,4,24,1024]{3,2,1,0:T(8,128)S(1)} %fusion.153, f32[4,4,32,1024]{3,2,1,0:T(8,128)S(1)} %get-tuple-element.13, f32[4,20,1024]{2,1,0:T(8,128)S(1)} %slice_bitcast_fusion.4, f32[4,20,1024]{2,1,0:T(8,128)S(1)} %slice_bitcast_fusion.5, ...), kind=kLoop, calls=%fused_computation.216 | loop fusion | flops 9830400 | bytes 9846864 | tf_op jit(solution)/shard_map/mul | solution.py:113
  156.0 0.1 slice.660
  156.1 3.1 %multiply_reduce_fusion.1 = f32[4,16,1024]{2,1,0:T(8,128)} fusion(f32[4,4,16,1024]{3,2,1,0:T(8,128)S(1)} %slice.623, f32[4,4,20,1024]{3,2,1,0:T(8,128)S(1)} %fusion.154, f32[4,4,32,1024]{3,2,1,0:T(8,128)S(1)} %get-tuple-element.11, f32[16]{0:T(128)S(1)} %slice.522, f32[4,16,1024]{2,1,0:T(8,128)S(1)} %slice_bitcast_fusion.14, ...), kind=kLoop, calls=%fused_computation.298 | loop fusion | flops 8323072 | bytes 7356480 | tf_op jit(solution)/shard_map/reduce_sum | solution.py:117
  159.3 0.0 copy-start.3
  159.3 3.1 %multiply_reduce_fusion = f32[4,16,1024]{2,1,0:T(8,128)} fusion(f32[4,4,16,1024]{3,2,1,0:T(8,128)S(1)} %slice.660, f32[4,4,20,1024]{3,2,1,0:T(8,128)S(1)} %fusion.152, f32[4,4,32,1024]{3,2,1,0:T(8,128)S(1)} %get-tuple-element.13, f32[4,16,1024]{2,1,0:T(8,128)S(1)} %slice_bitcast_fusion.12, f32[4,16,1024]{2,1,0:T(8,128)S(1)} %slice_bitcast_fusion.13, ...), kind=kLoop, calls=%fused_computation.296 | loop fusion | flops 8323072 | bytes 7356480 | tf_op jit(solution)/shard_map/reduce_sum | solution.py:117
  162.4 0.0 all-reduce.19.cloned.1.call-update
  162.4 0.0 copy-done.3
  162.4 75.3 %all-reduce.19.cloned.1.call-done = (f32[1,1,4,16,1024]{4,3,2,1,0:T(8,128)}, f32[1,1,4,16,1024]{4,3,2,1,0:T(8,128)}) async-done(((f32[1,1,4,16,1024]{4,3,2,1,0:T(8,128)}, f32[1,1,4,16,1024]{4,3,2,1,0:T(8,128)}), (f32[1,1,4,16,1024]{4,3,2,1,0:T(8,128)}, f32[1,1,4,16,1024]{4,3,2,1,0:T(8,128)})) %all-reduce.19.cloned.1.call-update) | async-done | bytes 524304 | tf_op jit(solution)/shard_map/psum | solution.py:116
  237.7 1.9 maximum_multiply_fusion
  (20 shorter events, 0.5 us)
Async XLA Ops:
  6.5 5.8 %copy-start.4 = (s32[4]{0:T(128)S(1)}, s32[4]{0:T(128)}, u32[]{:S(2)}) copy-start(s32[4]{0:T(128)} %param.10) | copy-start | bytes 52
  6.5 56.6 %all-gather.5.cloned.1.call-start = ((), (), s32[]{:S(2)}) async-start(), calls=%async_computation | async-start | bytes 2359296 | tf_op jit(solution)/shard_map/all_gather | solution.py:15
  11.2 101.7 %all-gather.7.cloned.1.call-start = ((), (), s32[]{:S(2)}) async-start(), calls=%async_computation.1 | async-start | bytes 2359296 | tf_op jit(solution)/shard_map/all_gather | solution.py:15
  11.9 225.8 %all-reduce.19.cloned.1.call-start = ((), (), s32[]{:S(2)}) async-start(), calls=%async_computation.2 | async-start | bytes 1048576 | tf_op jit(solution)/shard_map/psum | solution.py:116
  64.9 49.8 %copy-start = (f32[4,16,1024]{2,1,0:T(8,128)S(1)}, f32[4,16,1024]{2,1,0:T(8,128)}, u32[]{:S(2)}) copy-start(f32[4,16,1024]{2,1,0:T(8,128)} %param.7) | copy-start | bytes 786436
  64.9 49.8 %copy-start.1 = (f32[16,1024]{1,0:T(8,128)S(1)}, f32[16,1024]{1,0:T(8,128)}, u32[]{:S(2)}) copy-start(f32[16,1024]{1,0:T(8,128)} %param.8) | copy-start | bytes 196612
  114.9 8.8 %collective-permute-start = (f32[9,8,1024]{2,1,0:T(8,128)S(1)}, f32[9,8,1024]{2,1,0:T(8,128)S(1)}, u32[]{:S(2)}, u32[]{:S(2)}) collective-permute-start(f32[9,8,1024]{2,1,0:T(8,128)S(1)} %get-tuple-element.15), channel_id=1, source_target_pairs={{0,1},{1,2},{2,3},{4,5},{5,6},{6,7},{8,9},{9,10},{10,11},{12,13},{... | collective-permute-start | bytes 884744 | tf_op jit(solution)/shard_map/ppermute | solution.py:27
  116.2 7.5 %collective-permute-start.1 = (f32[9,8,1024]{2,1,0:T(8,128)S(1)}, f32[9,8,1024]{2,1,0:T(8,128)S(1)}, u32[]{:S(2)}, u32[]{:S(2)}) collective-permute-start(f32[9,8,1024]{2,1,0:T(8,128)S(1)} %get-tuple-element.16), channel_id=1, source_target_pairs={{1,0},{2,1},{3,2},{5,4},{6,5},{7,6},{9,8},{10,9},{11,10},{13,12},{... | collective-permute-start | bytes 884744 | tf_op jit(solution)/shard_map/ppermute | solution.py:29
  117.5 6.2 %collective-permute-start.2 = (f32[9,8,1024]{2,1,0:T(8,128)S(1)}, f32[9,8,1024]{2,1,0:T(8,128)S(1)}, u32[]{:S(2)}, u32[]{:S(2)}) collective-permute-start(f32[9,8,1024]{2,1,0:T(8,128)S(1)} %get-tuple-element.17), channel_id=1, source_target_pairs={{0,1},{1,2},{2,3},{4,5},{5,6},{6,7},{8,9},{9,10},{10,11},{12,13},{... | collective-permute-start | bytes 884744 | tf_op jit(solution)/shard_map/ppermute | solution.py:27
  122.3 4.7 %collective-permute-start.3 = (f32[9,8,1024]{2,1,0:T(8,128)S(1)}, f32[9,8,1024]{2,1,0:T(8,128)S(1)}, u32[]{:S(2)}, u32[]{:S(2)}) collective-permute-start(f32[9,8,1024]{2,1,0:T(8,128)S(1)} %get-tuple-element.18), channel_id=1, source_target_pairs={{1,0},{2,1},{3,2},{5,4},{6,5},{7,6},{9,8},{10,9},{11,10},{13,12},{... | collective-permute-start | bytes 884744 | tf_op jit(solution)/shard_map/ppermute | solution.py:29
  127.3 0.7 copy-start.2
  159.3 3.1 %copy-start.3 = (s32[2]{0:T(128)S(1)}, s32[2]{0:T(128)}, u32[]{:S(2)}) copy-start(s32[2]{0:T(128)} %param.11) | copy-start | bytes 28
Sparse Core Ops, SparseCore 0:
  11.3 51.7 all-gather.4
  65.3 47.6 all-gather.6
  162.5 75.1 all-reduce.18
